TPU v7x, 32 devices: a whole 2x2x4 slice. The times are simulated.
32 devices in a mesh: dp: 8 (over z, x), tp: 4 (over y, core).
Axes of the slice: x: 2, y: 2, z: 4, core: 2. Of those that a mesh axis runs over, the one named last changes fastest.
Arguments:
- inputs: bfloat16 [2, 4096, 768], P(None, 'dp'), may hold values from -6 to 6
- cotangent: bfloat16 [2, 4096, 768], P(None, 'dp'), may hold values from -6 to 6
- item_ids: int32 [2, 4096], P(None, 'dp'), may hold values from 0 to 3584, as said below
- timestep: int32 [2, 8], P(None, 'dp'), may hold values from 0 to 999
- qkv_weight: float32 [768, 3, 768], P('dp', None, 'tp'), may hold values from -0.21875 to 0.21875
- out_weight: float32 [768, 768], P('tp', 'dp'), may hold values from -0.625 to 0.625
- up_weight: float32 [768, 3072], P('dp', 'tp'), may hold values from -0.21875 to 0.21875
- down_weight: float32 [3072, 768], P('tp', 'dp'), may hold values from -0.109375 to 0.109375
- norm_params: float32 [4, 768], P(None, 'dp')
- qkv_first: float32 [768, 3, 768], P('dp', None, 'tp'), may hold values from -0.00061035156 to 0.00061035156
- out_first: float32 [768, 768], P('tp', 'dp'), may hold values from -0.00061035156 to 0.00061035156
- up_first: float32 [768, 3072], P('dp', 'tp'), may hold values from -0.00061035156 to 0.00061035156
- down_first: float32 [3072, 768], P('tp', 'dp'), may hold values from -0.00061035156 to 0.00061035156
- norm_first: float32 [4, 768], P(None, 'dp'), may hold values from -0.001953125 to 0.001953125
- qkv_second: float32 [768, 3, 768], P('dp', None, 'tp'), may hold values from 1.4122378e-10 to 5.6489513e-10
- out_second: float32 [768, 768], P('tp', 'dp'), may hold values from 1.4122378e-10 to 5.6489513e-10
- up_second: float32 [768, 3072], P('dp', 'tp'), may hold values from 1.4122378e-10 to 5.6489513e-10
- down_second: float32 [3072, 768], P('tp', 'dp'), may hold values from 1.4122378e-10 to 5.6489513e-10
- norm_second: float32 [4, 768], P(None, 'dp'), may hold values from 1.4122379e-09 to 5.6489515e-09
Outputs:
- block_out: bfloat16 [2, 4096, 768], P(None, 'dp')
- input_grad: float32 [2, 4096, 768], P(None, 'dp')
- grad_norm: float32 [], replicated
- qkv_new: float32 [768, 3, 768], P('dp', None, 'tp')
- qkv_first_new: float32 [768, 3, 768], P('dp', None, 'tp')
- qkv_second_new: float32 [768, 3, 768], P('dp', None, 'tp')
- out_new: float32 [768, 768], P('tp', 'dp')
- out_first_new: float32 [768, 768], P('tp', 'dp')
- out_second_new: float32 [768, 768], P('tp', 'dp')
- up_new: float32 [768, 3072], P('dp', 'tp')
- up_first_new: float32 [768, 3072], P('dp', 'tp')
- up_second_new: float32 [768, 3072], P('dp', 'tp')
- down_new: float32 [3072, 768], P('tp', 'dp')
- down_first_new: float32 [3072, 768], P('tp', 'dp')
- down_second_new: float32 [3072, 768], P('tp', 'dp')
- norm_new: float32 [4, 768], P(None, 'dp')
- norm_first_new: float32 [4, 768], P(None, 'dp')
- norm_second_new: float32 [4, 768], P(None, 'dp')
Inputs may be any that keep to these rules, and one draw needn't show every extreme that they name: `item_ids`: A token's id is the index, within its micro-batch, of its item's first token, so ids never decrease along a micro-batch; every block of 512 tokens of one index of dp starts a new item, so no item spans two blocks; an item has 1 to 512 tokens and in every draw some item has exactly 512.
All inputs are finite; a program needn't handle non-finite values.
Results may differ from a plain program's by a relative error of at most 0.009.
Values may be sent and summed in bfloat16 or wider, within the bound.
A program may use at most 128 MiB of HBM per device.

v0:
```python
from functools import partial
import math
import jax
import jax.numpy as jnp
from jax import lax
from jax.sharding import PartitionSpec as P

HEAD_DIM = 64
STEP = 10
norm_eps = 1e-05
clip_limit = 1.0
learn_rate = 0.02
beta_one = 0.9
beta_two = 0.999
adam_eps = 1e-08
weight_decay = 0.01


def time_embed(step_values, model_width):
    half_width = model_width // 2
    frequency = jnp.exp(
        jnp.arange(half_width, dtype=jnp.float32) * (-math.log(10000.0) / half_width)
    )
    angles = step_values.astype(jnp.float32)[..., None] * frequency
    return jnp.concatenate([jnp.sin(angles), jnp.cos(angles)], axis=-1)


def layer_norm(values, gain_row, bias_row):
    centre = values - jnp.mean(values, axis=-1, keepdims=True)
    spread = jnp.mean(centre * centre, axis=-1, keepdims=True)
    return centre * lax.rsqrt(spread + norm_eps) * gain_row + bias_row


def masked_scores(query_rows, key_rows, same_item, score_scale):
    scores = (
        jnp.einsum("thd,shd->hts", query_rows, key_rows, preferred_element_type=jnp.float32)
        * score_scale
    )
    return jnp.where(same_item, scores, -1e30)


def one_micro(gathered, stream_in, upstream, labels, embed_row):
    qkv_mat, out_mat, up_mat, down_mat, norm_rows = gathered
    tokens_here = stream_in.shape[0]
    local_width = out_mat.shape[0]
    heads_here = local_width // HEAD_DIM
    score_scale = 1.0 / math.sqrt(HEAD_DIM)
    split_shape = (tokens_here, heads_here, HEAD_DIM)
    norm_gains = norm_rows.astype(jnp.float32)
    gain_one = 1.0 + norm_gains[0]
    gain_two = 1.0 + norm_gains[2]
    stream = stream_in.astype(jnp.float32) + embed_row[None, :]
    normed_f, norm_one_back = jax.vjp(layer_norm, stream, gain_one, norm_gains[1])
    normed = normed_f.astype(jnp.bfloat16)
    triple = jnp.einsum("td,dje->jte", normed, qkv_mat, preferred_element_type=jnp.float32).astype(
        jnp.bfloat16
    )
    query_rows = triple[0].reshape(split_shape)
    key_rows = triple[1].reshape(split_shape)
    value_rows = triple[2].reshape(split_shape)
    same_item = (labels[:, None] == labels[None, :])[None]
    scores = masked_scores(query_rows, key_rows, same_item, score_scale)
    row_top = jnp.max(scores, axis=-1, keepdims=True)
    exp_scores = jnp.exp(scores - row_top)
    row_total = jnp.sum(exp_scores, axis=-1, keepdims=True)
    probs_soft = exp_scores / row_total
    log_total = row_top + jnp.log(row_total)
    context = (
        jnp.einsum(
            "hts,shd->thd",
            probs_soft.astype(jnp.bfloat16),
            value_rows,
            preferred_element_type=jnp.float32,
        )
        .reshape(tokens_here, local_width)
        .astype(jnp.bfloat16)
    )
    attn_out = lax.psum(jnp.dot(context, out_mat, preferred_element_type=jnp.float32), "tp")
    middle = stream + attn_out
    normed_two_f, norm_two_back = jax.vjp(layer_norm, middle, gain_two, norm_gains[3])
    normed_two = normed_two_f.astype(jnp.bfloat16)
    hidden_pre = jnp.dot(normed_two, up_mat, preferred_element_type=jnp.float32)
    hidden_f, gelu_back = jax.vjp(partial(jax.nn.gelu, approximate=False), hidden_pre)
    hidden = hidden_f.astype(jnp.bfloat16)
    branch = lax.psum(
        jnp.dot(hidden, down_mat, preferred_element_type=jnp.float32).astype(jnp.bfloat16), "tp"
    ).astype(jnp.float32)
    block_out = (middle + branch).astype(jnp.bfloat16)
    grad_down = jnp.einsum("tf,td->fd", hidden, upstream, preferred_element_type=jnp.float32)
    grad_hidden = jnp.einsum("td,fd->tf", upstream, down_mat, preferred_element_type=jnp.float32)
    grad_pre = gelu_back(grad_hidden)[0].astype(jnp.bfloat16)
    grad_up = jnp.einsum("td,tf->df", normed_two, grad_pre, preferred_element_type=jnp.float32)
    grad_normed_two = lax.psum(
        jnp.einsum("tf,df->td", grad_pre, up_mat, preferred_element_type=jnp.float32), "tp"
    )
    grad_middle_norm, grad_gain_two, grad_bias_two = norm_two_back(grad_normed_two)
    grad_middle = upstream.astype(jnp.float32) + grad_middle_norm
    grad_attn = grad_middle.astype(jnp.bfloat16)
    grad_outmat = jnp.einsum("tc,td->cd", context, grad_attn, preferred_element_type=jnp.float32)
    grad_context = (
        jnp.einsum("td,cd->tc", grad_attn, out_mat, preferred_element_type=jnp.float32)
        .astype(jnp.bfloat16)
        .reshape(split_shape)
    )
    probs_again = jnp.exp(masked_scores(query_rows, key_rows, same_item, score_scale) - log_total)
    grad_values = jnp.einsum(
        "hts,thd->shd",
        probs_again.astype(jnp.bfloat16),
        grad_context,
        preferred_element_type=jnp.float32,
    )
    grad_probs = jnp.einsum(
        "thd,shd->hts", grad_context, value_rows, preferred_element_type=jnp.float32
    )
    inner_sum = jnp.sum(grad_probs * probs_again, axis=-1, keepdims=True)
    grad_scores = (probs_again * (grad_probs - inner_sum)).astype(jnp.bfloat16)
    grad_query = (
        jnp.einsum("hts,shd->thd", grad_scores, key_rows, preferred_element_type=jnp.float32)
        * score_scale
    )
    grad_key = (
        jnp.einsum("hts,thd->shd", grad_scores, query_rows, preferred_element_type=jnp.float32)
        * score_scale
    )
    grad_triple = (
        jnp.stack([grad_query, grad_key, grad_values])
        .reshape(3, tokens_here, local_width)
        .astype(jnp.bfloat16)
    )
    grad_qkv = jnp.einsum("td,jte->dje", normed, grad_triple, preferred_element_type=jnp.float32)
    grad_normed = lax.psum(
        jnp.einsum("jte,dje->td", grad_triple, qkv_mat, preferred_element_type=jnp.float32).astype(
            jnp.bfloat16
        ),
        "tp",
    ).astype(jnp.float32)
    grad_stream_norm, grad_gain_one, grad_bias_one = norm_one_back(grad_normed)
    grad_input = grad_middle + grad_stream_norm
    grad_norms = jnp.stack([grad_gain_one, grad_bias_one, grad_gain_two, grad_bias_two])
    return (block_out, grad_input, (grad_qkv, grad_outmat, grad_up, grad_down, grad_norms))


def adam_step(weight, gradient, first_old, second_old):
    first_new = beta_one * first_old + (1.0 - beta_one) * gradient
    second_new = beta_two * second_old + (1.0 - beta_two) * gradient * gradient
    moment_one = first_new / (1.0 - beta_one**STEP)
    moment_two = second_new / (1.0 - beta_two**STEP)
    weight_new = weight - learn_rate * (
        moment_one / (jnp.sqrt(moment_two) + adam_eps) + weight_decay * weight
    )
    return (weight_new, first_new, second_new)


def local(
    inputs,
    cotangent,
    item_ids,
    timestep,
    qkv_weight,
    out_weight,
    up_weight,
    down_weight,
    norm_params,
    qkv_first,
    out_first,
    up_first,
    down_first,
    norm_first,
    qkv_second,
    out_second,
    up_second,
    down_second,
    norm_second,
):
    micro_count = inputs.shape[0]
    embeds = time_embed(timestep[:, 0], inputs.shape[2])
    qkv_low = qkv_weight.astype(jnp.bfloat16)
    out_low = out_weight.astype(jnp.bfloat16)
    up_low = up_weight.astype(jnp.bfloat16)
    down_low = down_weight.astype(jnp.bfloat16)
    norm_low = norm_params.astype(jnp.bfloat16)
    block_list = []
    input_list = []
    for number in range(micro_count):
        gathered = (
            lax.all_gather(qkv_low, "dp", axis=0, tiled=True),
            lax.all_gather(out_low, "dp", axis=1, tiled=True),
            lax.all_gather(up_low, "dp", axis=0, tiled=True),
            lax.all_gather(down_low, "dp", axis=1, tiled=True),
            lax.all_gather(norm_low, "dp", axis=1, tiled=True),
        )
        block_out, grad_input, grad_list = one_micro(
            gathered, inputs[number], cotangent[number], item_ids[number], embeds[number]
        )
        owned_grads = (
            lax.psum_scatter(grad_list[0], "dp", scatter_dimension=0, tiled=True),
            lax.psum_scatter(grad_list[1], "dp", scatter_dimension=1, tiled=True),
            lax.psum_scatter(grad_list[2], "dp", scatter_dimension=0, tiled=True),
            lax.psum_scatter(grad_list[3], "dp", scatter_dimension=1, tiled=True),
            lax.psum_scatter(grad_list[4], "dp", scatter_dimension=1, tiled=True),
        )
        if number == 0:
            totals = tuple(owned_grads)
        else:
            totals = tuple((left + right for left, right in zip(totals, owned_grads)))
        block_list.append(block_out)
        input_list.append(grad_input)
    own_squares = jnp.sum(totals[0] * totals[0]) + jnp.sum(totals[1] * totals[1])
    own_squares = own_squares + jnp.sum(totals[2] * totals[2]) + jnp.sum(totals[3] * totals[3])
    norm_squares = jnp.sum(totals[4] * totals[4])
    own_squares = own_squares + jnp.where(
        lax.axis_index("tp") == 0, norm_squares, jnp.zeros_like(norm_squares)
    )
    grad_norm = jnp.sqrt(lax.psum(own_squares, ("dp", "tp")))
    factor = jnp.minimum(1.0, clip_limit / (grad_norm + 1e-06))
    weights = (qkv_weight, out_weight, up_weight, down_weight, norm_params)
    firsts = (qkv_first, out_first, up_first, down_first, norm_first)
    seconds = (qkv_second, out_second, up_second, down_second, norm_second)
    result = [
        adam_step(weights[index], totals[index] * factor, firsts[index], seconds[index])
        for index in range(5)
    ]
    return (
        jnp.stack(block_list),
        jnp.stack(input_list),
        grad_norm,
        result[0][0],
        result[0][1],
        result[0][2],
        result[1][0],
        result[1][1],
        result[1][2],
        result[2][0],
        result[2][1],
        result[2][2],
        result[3][0],
        result[3][1],
        result[3][2],
        result[4][0],
        result[4][1],
        result[4][2],
    )


def solution(mesh):
    return jax.shard_map(
        local,
        mesh=mesh,
        in_specs=(
            P(None, "dp", None),
            P(None, "dp", None),
            P(None, "dp"),
            P(None, "dp"),
            P("dp", None, "tp"),
            P("tp", "dp"),
            P("dp", "tp"),
            P("tp", "dp"),
            P(None, "dp"),
            P("dp", None, "tp"),
            P("tp", "dp"),
            P("dp", "tp"),
            P("tp", "dp"),
            P(None, "dp"),
            P("dp", None, "tp"),
            P("tp", "dp"),
            P("dp", "tp"),
            P("tp", "dp"),
            P(None, "dp"),
        ),
        out_specs=(
            P(None, "dp", None),
            P(None, "dp", None),
            P(),
            P("dp", None, "tp"),
            P("dp", None, "tp"),
            P("dp", None, "tp"),
            P("tp", "dp"),
            P("tp", "dp"),
            P("tp", "dp"),
            P("dp", "tp"),
            P("dp", "tp"),
            P("dp", "tp"),
            P("tp", "dp"),
            P("tp", "dp"),
            P("tp", "dp"),
            P(None, "dp"),
            P(None, "dp"),
            P(None, "dp"),
        ),
        check_vma=False,
    )
```

profile of v0, /device:TPU:0, one launch (start us, length us, event | category | flops | bytes accessed | tf_op | source)
XLA Modules:
  0.0 723.9 jit_solution(8021237277195858394)
XLA Ops:
  9.0 1.8 fusion.30
  10.9 1.2 fusion.37
  12.2 22.2 %all-gather = bf16[8,96,4]{1,2,0:T(4,128)(2,1)S(1)} all-gather(bf16[1,96,4]{1,2,0:T(4,128)(2,1)S(1)} %convert_bitcast_fusion.2), channel_id=1, replica_groups=mesh['dp'=8,'tp'=4] {'dp'}, dimensions={0}, use_global_device_ids=true | all-gather | bytes 6912 | tf_op jit(solution)/shard_map/all_gather | solution.py:190
  35.3 35.3 %all_gather.21 = bf16[768,3,192]{2,1,0:T(4,128)(2,1)S(1)} all-gather(bf16[96,3,192]{2,1,0:T(4,128)(2,1)S(1)} %copy.82), channel_id=1, replica_groups=mesh['dp'=8,'tp'=4] {'dp'}, dimensions={0}, use_global_device_ids=true | all-gather | bytes 995328 | tf_op jit(solution)/shard_map/all_gather | solution.py:186
  70.6 2.1 copy.83
  72.6 2.0 fusion.107
  76.1 0.9 broadcast_compare_fusion.1
  77.2 31.1 %all_gather.22 = bf16[192,768]{0,1:T(8,128)(2,1)S(1)} all-gather(bf16[192,96]{0,1:T(8,128)(2,1)S(1)} %copy.85), channel_id=1, replica_groups=mesh['dp'=8,'tp'=4] {'dp'}, dimensions={1}, use_global_device_ids=true | all-gather | bytes 331776 | tf_op jit(solution)/shard_map/all_gather | solution.py:187
  108.3 2.0 fusion.110
  112.6 1.2 copy-done
  114.5 1.6 fusion.133
  118.8 1.6 fusion.134
  120.4 1.6 convert_element_type.172
  122.1 1.6 convert_element_type.174
  124.4 64.3 %all-reduce.9.cloned.1.call-done = (f32[512,768]{1,0:T(8,128)}, f32[512,768]{1,0:T(8,128)}) async-done(((f32[512,768]{1,0:T(8,128)}, f32[512,768]{1,0:T(8,128)}), (f32[512,768]{1,0:T(8,128)}, f32[512,768]{1,0:T(8,128)})) %all-reduce.9.cloned.1.call-update) | async-done | bytes 3145744 | tf_op jit(solution)/shard_map/psum | solution.py:78
  188.7 3.0 fusion.123
  194.6 7.6 %multiply_convert_fusion.3 = (bf16[512,768]{1,0:T(8,128)(2,1)}, f32[512,768]{1,0:T(8,128)}, f32[512,768]{1,0:T(8,128)}) fusion(bf16[768,768]{1,0:T(8,128)(2,1)} %all-gather.4.cloned.1.call-done, f32[512,768]{1,0:T(8,128)} %copy-done.8, f32[768]{0:T(1024)} %get-tuple-element.39, f32[768]{0:T(1024)} %get-tuple-element.38, f32[512]{0:T(512)} %fusion.99, ...), kind=kOutput, calls=%fused_computation.98 | convolution fusion | flops 631504896 | bytes 6694912 | tf_op jit(solution)/shard_map/dot_general | solution.py:82
  202.2 4.3 all-gather.6.cloned.1.call-done
  206.5 3.6 add_convert_fusion.1
  210.1 0.9 copy-done.144
  211.0 2.0 fusion.135
  213.1 5.0 multiply_convert_fusion.2
  218.1 1.1 add_convert_fusion
  219.2 0.9 copy-done.57
  220.1 2.0 fusion.136
  222.3 1.3 log_add_fusion.1
  224.3 3.4 convolution_convert_fusion.1
  227.7 1.8 convolution_convert_fusion
  229.5 59.9 %all-reduce.7.cloned.1.call-done = (f32[512,768]{1,0:T(8,128)}, f32[512,768]{1,0:T(8,128)}) async-done(((f32[512,768]{1,0:T(8,128)}, f32[512,768]{1,0:T(8,128)}), (f32[512,768]{1,0:T(8,128)}, f32[512,768]{1,0:T(8,128)})) %all-reduce.7.cloned.1.call-update) | async-done | bytes 3145744 | tf_op jit(solution)/shard_map/psum | solution.py:93
  289.4 4.7 multiply_reduce_fusion.3
  294.2 1.4 fusion.120
  298.2 1.0 copy-done.1
  307.9 1.7 bitcast_convert_fusion.1
  309.7 1.7 bitcast_convert_fusion
  311.8 1.0 copy-done.10
  312.8 3.5 fusion.112
  316.8 0.9 copy-done.23
  318.2 1.2 copy.110
  319.4 61.3 %all-reduce.11.cloned.1.call-done = (bf16[512,768]{1,0:T(8,128)(2,1)}, bf16[512,768]{1,0:T(8,128)(2,1)}, bf16[512,768]{1,0:T(8,128)(2,1)}, bf16[512,768]{1,0:T(8,128)(2,1)}) async-done(((bf16[512,768]{1,0:T(8,128)(2,1)}, bf16[512,768]{1,0:T(8,128)(2,1)}, bf16[512,768]{1,0:T(8,128)(2,1)}, bf16[512,768]{1,0:T(8,128)(2,1)}), (bf16[512,768]{1,0:T(8,128)(2,1)}, bf16[512,768]{1,0:T(8,128)(2,1)}, ...) | async-done | bytes 3145744 | tf_op jit(solution)/shard_map/psum | solution.py:85
  380.8 2.5 fusion.9
  383.5 2.5 fusion.12
  386.1 0.9 copy.112
  387.2 4.4 convolution_add_fusion.1
  391.7 2.3 fusion.78
  394.1 2.3 convolution_add_fusion
  397.3 2.1 fusion.71
  399.5 2.5 convolution_add_fusion.2
  402.1 1.0 copy.111
  403.8 2.8 add_bitcast_fusion.1
  407.6 1.9 pad_maximum_fusion
  410.6 0.9 copy-done.55
  411.7 37.1 %reduce-scatter.18.cloned.1.call-done = f32[96,4]{1,0:T(8,128)} async-done(((f32[768,4]{1,0:T(8,128)}), f32[96,4]{1,0:T(8,128)}) %reduce-scatter.18.cloned.1.call-update) | async-done | bytes 1552
  448.8 0.9 copy.113
  450.9 70.0 %reduce-scatter.12.cloned.1.call-done = f32[96,768]{1,0:T(8,128)} async-done(((f32[768,768]{1,0:T(8,128)}), f32[96,768]{1,0:T(8,128)}) %reduce-scatter.12.cloned.1.call-update) | async-done | bytes 294928 | tf_op jit(solution)/shard_map/reduce_scatter | solution.py:198
  521.0 1.6 multiply_reduce_fusion.9
  522.6 70.3 %reduce-scatter.14.cloned.1.call-done = f32[768,96]{0,1:T(8,128)} async-done(((f32[768,768]{0,1:T(8,128)}), f32[768,96]{0,1:T(8,128)}) %reduce-scatter.14.cloned.1.call-update) | async-done | bytes 294928 | tf_op jit(solution)/shard_map/reduce_scatter | solution.py:199
  593.0 1.6 multiply_reduce_fusion.8
  594.6 70.2 %reduce-scatter.10.cloned.1.call-done = f32[96,3,192]{2,0,1:T(8,128)} async-done(((f32[768,3,192]{2,0,1:T(8,128)}), f32[96,3,192]{2,0,1:T(8,128)}) %reduce-scatter.10.cloned.1.call-update) | async-done | bytes 221200 | tf_op jit(solution)/shard_map/reduce_scatter | solution.py:196
  664.8 1.6 multiply_reduce_fusion.10
  669.1 1.3 pad_maximum_fusion.1
  670.4 39.6 %psum.71 = f32[]{:T(128)} all-reduce(f32[]{:T(128)S(6)} %add.323), channel_id=1, replica_groups=mesh['dp'=8,'tp'=4] {'dp','tp'}, use_global_device_ids=true, to_apply=%region_53.54 | all-reduce | flops 1 | bytes 8 | tf_op jit(solution)/shard_map/psum | solution.py:214
  712.2 1.1 multiply_subtract_fusion
  713.2 1.1 multiply_subtract_fusion.1
  714.3 1.1 multiply_subtract_fusion.2
  (377 shorter events, 31.9 us)
Async XLA Ops:
  8.0 180.7 %all-reduce.9.cloned.1.call-start = ((), (), s32[]{:S(2)}) async-start(), calls=%async_computation.13 | async-start | bytes 6291456 | tf_op jit(solution)/shard_map/psum | solution.py:78
  9.0 26.1 %copy-start.38 = (f32[96,3,192]{2,0,1:T(8,128)S(1)}, f32[96,3,192]{2,0,1:T(8,128)}, u32[]{:S(2)}) copy-start(f32[96,3,192]{2,0,1:T(8,128)} %param.23) | copy-start | bytes 663556
  10.8 61.8 %copy-start.85 = (f32[512]{0:T(512)}, f32[512]{0:T(512)S(1)}, u32[]{:S(2)}) copy-start(f32[512]{0:T(512)S(1)} %get-tuple-element.109) | copy-start | bytes 6148
  10.9 97.4 %copy-start.83 = (f32[512]{0:T(512)}, f32[512]{0:T(512)S(1)}, u32[]{:S(2)}) copy-start(f32[512]{0:T(512)S(1)} %get-tuple-element.108) | copy-start | bytes 6148
  12.1 22.4 %copy-start.118 = (f32[512]{0:T(512)}, f32[512]{0:T(512)S(1)}, u32[]{:S(2)}) copy-start(f32[512]{0:T(512)S(1)} %get-tuple-element.32) | copy-start | bytes 6148
  12.1 60.5 %copy-start.104 = (f32[512]{0:T(512)}, f32[512]{0:T(512)S(1)}, u32[]{:S(2)}) copy-start(f32[512]{0:T(512)S(1)} %fusion.98) | copy-start | bytes 6148
  35.1 37.5 %copy-start.136 = (f32[768]{0:T(1024)}, f32[768]{0:T(1024)S(1)}, u32[]{:S(2)}) copy-start(f32[768]{0:T(1024)S(1)} %get-tuple-element.40) | copy-start | bytes 9220
  35.1 73.2 %copy-start.75 = (f32[768]{0:T(1024)}, f32[768]{0:T(1024)S(1)}, u32[]{:S(2)}) copy-start(f32[768]{0:T(1024)S(1)} %get-tuple-element.41) | copy-start | bytes 9220
  74.7 33.6 %copy-start.120 = (f32[512]{0:T(512)S(1)}, f32[512]{0:T(512)}, u32[]{:S(2)}) copy-start(f32[512]{0:T(512)} %get-tuple-element.33) | copy-start | bytes 6148
  75.5 35.8 %copy-start.32 = (bf16[1,512,192]{1,2,0:T(8,128)(2,1)}, bf16[1,512,192]{1,2,0:T(8,128)(2,1)S(1)}, u32[]{:S(2)}) copy-start(bf16[1,512,192]{1,2,0:T(8,128)(2,1)S(1)} %get-tuple-element.84) | copy-start | bytes 589828
  75.5 35.8 %copy-start.34 = (bf16[1,512,192]{1,2,0:T(8,128)(2,1)}, bf16[1,512,192]{1,2,0:T(8,128)(2,1)S(1)}, u32[]{:S(2)}) copy-start(bf16[1,512,192]{1,2,0:T(8,128)(2,1)S(1)} %get-tuple-element.83) | copy-start | bytes 589828
  110.5 5.5 copy-start.28
  110.5 5.5 copy-start.30
  110.6 6.7 copy-start.45
  120.4 74.2 %all-gather.4.cloned.1.call-start = ((), (), s32[]{:S(2)}) async-start(), calls=%async_computation.5 | async-start | bytes 1327104 | tf_op jit(solution)/shard_map/all_gather | solution.py:188
  122.1 84.4 %all-gather.6.cloned.1.call-start = ((), (), s32[]{:S(2)}) async-start(), calls=%async_computation.6 | async-start | bytes 1327104 | tf_op jit(solution)/shard_map/all_gather | solution.py:189
  123.8 165.6 %all-reduce.7.cloned.1.call-start = ((), (), s32[]{:S(2)}) async-start(), calls=%async_computation.12 | async-start | bytes 6291456 | tf_op jit(solution)/shard_map/psum | solution.py:93
  206.5 4.5 copy-start.143
  213.0 5.0 copy-start.12
  213.0 5.0 copy-start.141
  222.1 158.7 %all-reduce.11.cloned.1.call-start = ((), (), s32[]{:S(2)}) async-start(), calls=%async_computation.14 | async-start | bytes 6291456 | tf_op jit(solution)/shard_map/psum | solution.py:85
  289.4 4.7 copy-start.125
  289.4 4.8 copy-start.123
  289.4 4.8 copy-start.6
  289.4 4.8 copy-start.9
  289.4 4.8 copy-start.26
  289.4 4.8 copy-start.27
  289.4 4.8 copy-start.81
  289.4 4.8 copy-start.90
  289.4 4.8 copy-start.93
  289.4 4.8 copy-start.98
  289.4 4.8 copy-start.115
  297.3 5.8 copy-start.22
  301.8 5.5 copy-start.68
  302.4 4.9 copy-start.69
  311.4 4.9 copy-start.131
  311.5 4.9 copy-start.130
  311.5 4.9 copy-start.129
  311.5 4.9 copy-start.128
  311.5 4.9 copy-start.25
  311.5 4.9 copy-start.52
  311.5 90.5 %reduce-scatter.16.cloned.1.call-start = ((), (), s32[]{:S(2)}) async-start(), calls=%async_computation.10 | async-start | bytes 884736
  318.1 62.6 %copy-start.3 = (bf16[2,512,768]{2,1,0:T(8,128)(2,1)S(1)}, bf16[2,512,768]{2,1,0:T(8,128)(2,1)}, u32[]{:S(2)}) copy-start(bf16[2,512,768]{2,1,0:T(8,128)(2,1)} %param.19) | copy-start | bytes 4718596
  318.1 62.6 %copy-start.76 = (f32[768]{0:T(1024)S(1)}, f32[768]{0:T(1024)}, u32[]{:S(2)}) copy-start(f32[768]{0:T(1024)} %copy-done.75) | copy-start | bytes 9220
  318.2 62.6 %copy-start.84 = (f32[512]{0:T(512)S(1)}, f32[512]{0:T(512)}, u32[]{:S(2)}) copy-start(f32[512]{0:T(512)} %copy-done.83) | copy-start | bytes 6148
  318.2 62.6 %copy-start.86 = (f32[512]{0:T(512)S(1)}, f32[512]{0:T(512)}, u32[]{:S(2)}) copy-start(f32[512]{0:T(512)} %copy-done.85) | copy-start | bytes 6148
  319.4 129.4 %reduce-scatter.18.cloned.1.call-start = ((), (), s32[]{:S(2)}) async-start(), calls=%async_computation.11 | async-start | bytes 442368
  387.1 133.9 %reduce-scatter.12.cloned.1.call-start = ((), (), s32[]{:S(2)}) async-start(), calls=%async_computation.8 | async-start | bytes 2654208 | tf_op jit(solution)/shard_map/reduce_scatter | solution.py:198
  391.6 201.4 %reduce-scatter.14.cloned.1.call-start = ((), (), s32[]{:S(2)}) async-start(), calls=%async_computation.9 | async-start | bytes 2654208 | tf_op jit(solution)/shard_map/reduce_scatter | solution.py:199
  396.3 268.4 %reduce-scatter.10.cloned.1.call-start = ((), (), s32[]{:S(2)}) async-start(), calls=%async_computation.7 | async-start | bytes 2654208 | tf_op jit(solution)/shard_map/reduce_scatter | solution.py:196
  669.0 41.7 %copy-start.135 = (f32[4,96]{1,0:T(4,128)S(1)}, f32[4,96]{1,0:T(4,128)}, u32[]{:S(2)}) copy-start(f32[4,96]{1,0:T(4,128)} %param.27) | copy-start | bytes 4612
  669.0 41.7 %copy-start.139 = (f32[4,96]{1,0:T(4,128)S(1)}, f32[4,96]{1,0:T(4,128)}, u32[]{:S(2)}) copy-start(f32[4,96]{1,0:T(4,128)} %param.32) | copy-start | bytes 4612
  669.0 41.7 %copy-start.140 = (f32[4,96]{1,0:T(4,128)S(1)}, f32[4,96]{1,0:T(4,128)}, u32[]{:S(2)}) copy-start(f32[4,96]{1,0:T(4,128)} %param.37) | copy-start | bytes 4612
  669.0 42.3 %copy-start.59 = (f32[192,96]{1,0:T(8,128)S(1)}, f32[192,96]{1,0:T(8,128)}, u32[]{:S(2)}) copy-start(f32[192,96]{1,0:T(8,128)} %param.24) | copy-start | bytes 221188
  669.0 42.3 %copy-start.77 = (f32[192,96]{1,0:T(8,128)S(1)}, f32[192,96]{1,0:T(8,128)}, u32[]{:S(2)}) copy-start(f32[192,96]{1,0:T(8,128)} %param.29) | copy-start | bytes 221188
  669.1 42.3 %copy-start.78 = (f32[192,96]{1,0:T(8,128)S(1)}, f32[192,96]{1,0:T(8,128)}, u32[]{:S(2)}) copy-start(f32[192,96]{1,0:T(8,128)} %param.34) | copy-start | bytes 221188
  669.1 43.0 %copy-start.36 = (f32[768,96]{0,1:T(8,128)S(1)}, f32[768,96]{0,1:T(8,128)}, u32[]{:S(2)}) copy-start(f32[768,96]{0,1:T(8,128)} %param.26) | copy-start | bytes 884740
  669.1 43.0 %copy-start.41 = (f32[768,96]{0,1:T(8,128)S(1)}, f32[768,96]{0,1:T(8,128)}, u32[]{:S(2)}) copy-start(f32[768,96]{0,1:T(8,128)} %reduce-scatter.14.cloned.1.call-done) | copy-start | bytes 884740
  669.1 43.0 %copy-start.60 = (f32[768,96]{0,1:T(8,128)S(1)}, f32[768,96]{0,1:T(8,128)}, u32[]{:S(2)}) copy-start(f32[768,96]{0,1:T(8,128)} %param.31) | copy-start | bytes 884740
  669.1 43.0 %copy-start.61 = (f32[768,96]{0,1:T(8,128)S(1)}, f32[768,96]{0,1:T(8,128)}, u32[]{:S(2)}) copy-start(f32[768,96]{0,1:T(8,128)} %param.36) | copy-start | bytes 884740
  670.4 42.8 %copy-start.37 = (f32[96,768]{1,0:T(8,128)S(1)}, f32[96,768]{1,0:T(8,128)}, u32[]{:S(2)}) copy-start(f32[96,768]{1,0:T(8,128)} %param.25) | copy-start | bytes 884740
  670.4 42.8 %copy-start.40 = (f32[96,768]{1,0:T(8,128)S(1)}, f32[96,768]{1,0:T(8,128)}, u32[]{:S(2)}) copy-start(f32[96,768]{1,0:T(8,128)} %reduce-scatter.12.cloned.1.call-done) | copy-start | bytes 884740
  670.4 42.8 %copy-start.62 = (f32[96,768]{1,0:T(8,128)S(1)}, f32[96,768]{1,0:T(8,128)}, u32[]{:S(2)}) copy-start(f32[96,768]{1,0:T(8,128)} %param.30) | copy-start | bytes 884740
  670.4 42.8 %copy-start.63 = (f32[96,768]{1,0:T(8,128)S(1)}, f32[96,768]{1,0:T(8,128)}, u32[]{:S(2)}) copy-start(f32[96,768]{1,0:T(8,128)} %param.35) | copy-start | bytes 884740
  (91 other events, 183.2 us)
Sparse Core Ops, SparseCore 0:
  120.5 68.1 all-reduce.8
  222.2 67.1 all-reduce.6
  311.6 69.1 all-reduce.10
Sparse Core Ops, SparseCore 1:
  123.6 40.9 all-gather.3
  166.6 39.9 all-gather.5
  319.5 62.4 reduce-scatter.15
  387.2 61.6 reduce-scatter.17
  452.7 68.2 reduce-scatter.11
  524.9 68.0 reduce-scatter.13
  596.7 68.0 reduce-scatter.9
where the time goes:
time: 731 us; the launch traced here: 724 us
  waiting for transfers between devices  438 us (60%)
  blocking collectives  128 us (18%)
  matrix products  63.2 us (9%)
  other arithmetic  47.9 us (7%)
  local copies, waits for them, and re-layouts  22.8 us (3%)
  between operations  22.4 us (3%)
    reduce_scatter x1, waiting for transfers between devices, local(): lax.psum_scatter(grad_list[3], 'dp', scatter_dimension=1, tiled=True)  70.3 us
    reduce_scatter x1, waiting for transfers between devices, local(): lax.psum_scatter(grad_list[0], 'dp', scatter_dimension=0, tiled=True)  70.2 us
    reduce_scatter x1, waiting for transfers between devices, local(): lax.psum_scatter(grad_list[2], 'dp', scatter_dimension=0, tiled=True)  70 us
    psum x1, waiting for transfers between devices, one_micro(): lax.psum(jnp.dot(context, out_mat, preferred_element_type=jnp.float32), '...  64.3 us
    psum x1, waiting for transfers between devices, one_micro(): lax.psum(jnp.dot(hidden, down_mat, preferred_element_type=jnp.float32).as...  61.3 us
    psum x1, waiting for transfers between devices, one_micro(): lax.psum(jnp.einsum('tf,df->td', grad_pre, up_mat, preferred_element_type...  59.9 us
    psum x1, blocking collectives, local(): grad_norm = jnp.sqrt(lax.psum(own_squares, ('dp', 'tp')))  39.6 us
    unnamed x12, waiting for transfers between devices  37.3 us
  transfers between devices with their start and end apart: 10, of which 8 were waited for; matrix products, arithmetic and copies ran while one was open for 8% of the time, Pallas kernels for 0%

commit v1 on v0

--- a/solution.py
+++ b/solution.py
@@ -75,7 +75,9 @@
         .reshape(tokens_here, local_width)
         .astype(jnp.bfloat16)
     )
-    attn_out = lax.psum(jnp.dot(context, out_mat, preferred_element_type=jnp.float32), "tp")
+    attn_out = jnp.sum(
+        lax.all_gather(jnp.dot(context, out_mat, preferred_element_type=jnp.float32), "tp"), axis=0
+    )
     middle = stream + attn_out
     normed_two_f, norm_two_back = jax.vjp(layer_norm, middle, gain_two, norm_gains[3])
     normed_two = normed_two_f.astype(jnp.bfloat16)

time: 731 us -> 880 us (1.20)
  waiting for transfers between devices: 438 us -> 575 us
  other arithmetic: 47.9 us -> 58.3 us
    all_gather x0 -> x2, waiting for transfers between devices: none -> 76.5 us  [one_micro(): lax.all_gather(jnp.dot(context, out_mat, preferred_element_type=jnp.float...]
    psum x1 -> x0, waiting for transfers between devices: 64.3 us -> none  [one_micro(): lax.psum(jnp.dot(context, out_mat, preferred_element_type=jnp.float32), '...]
    unnamed x12 -> x13, waiting for transfers between devices: 37.3 us -> 99.3 us
    all_gather x1, waiting for transfers between devices: 0.01 us -> 33.6 us  [local(): lax.all_gather(up_low, 'dp', axis=0, tiled=True)]
    all_gather x1, waiting for transfers between devices: 4.33 us -> 34.3 us  [local(): lax.all_gather(down_low, 'dp', axis=1, tiled=True)]
    reduce_sum x0 -> x2, other arithmetic: none -> 9.04 us  [one_micro(): jnp.sum(lax.all_gather(jnp.dot(context, out_mat, preferred_element_type=j...]
    unnamed x295 -> x285, local copies, waits for them, and re-layouts: 19.1 us -> 19.9 us
  transfers between devices with their start and end apart: 10 -> 11, of which waited for: 8 -> 11; matrix products, arithmetic and copies ran while one was open for 8% -> 9% of each run, Pallas kernels for 0% -> 0%
where the time goes in v1:
time: 880 us; the launch traced here: 872 us
  waiting for transfers between devices  575 us (65%)
  blocking collectives  128 us (15%)
  matrix products  64.6 us (7%)
  other arithmetic  58.3 us (7%)
  local copies, waits for them, and re-layouts  23.7 us (3%)
  between operations  20.9 us (2%)
    unnamed x13, waiting for transfers between devices  99.3 us
    all_gather x2, waiting for transfers between devices, one_micro(): lax.all_gather(jnp.dot(context, out_mat, preferred_element_type=jnp.float...  76.5 us
    reduce_scatter x1, waiting for transfers between devices, local(): lax.psum_scatter(grad_list[0], 'dp', scatter_dimension=0, tiled=True)  70.2 us
    reduce_scatter x1, waiting for transfers between devices, local(): lax.psum_scatter(grad_list[3], 'dp', scatter_dimension=1, tiled=True)  70.1 us
    reduce_scatter x1, waiting for transfers between devices, local(): lax.psum_scatter(grad_list[2], 'dp', scatter_dimension=0, tiled=True)  69.8 us
    psum x1, waiting for transfers between devices, one_micro(): lax.psum(jnp.dot(hidden, down_mat, preferred_element_type=jnp.float32).as...  61.1 us
    psum x1, waiting for transfers between devices, one_micro(): lax.psum(jnp.einsum('tf,df->td', grad_pre, up_mat, preferred_element_type...  60.2 us
    psum x1, blocking collectives, local(): grad_norm = jnp.sqrt(lax.psum(own_squares, ('dp', 'tp')))  39.5 us
  transfers between devices with their start and end apart: 11, of which 11 were waited for; matrix products, arithmetic and copies ran while one was open for 9% of the time, Pallas kernels for 0%

profile of v1, /device:TPU:0, one launch (start us, length us, event | category | flops | bytes accessed | tf_op | source)
XLA Modules:
  0.0 872.0 jit_solution(12331755158194118148)
XLA Ops:
  8.2 1.8 fusion.30
  10.0 1.2 fusion.37
  11.2 22.2 %all-gather.2 = bf16[8,96,4]{1,2,0:T(4,128)(2,1)S(1)} all-gather(bf16[1,96,4]{1,2,0:T(4,128)(2,1)S(1)} %convert_bitcast_fusion.2), channel_id=1, replica_groups=mesh['dp'=8,'tp'=4] {'dp'}, dimensions={0}, use_global_device_ids=true | all-gather | bytes 6912 | tf_op jit(solution)/shard_map/all_gather | solution.py:192
  34.3 35.3 %all_gather.33 = bf16[768,3,192]{2,1,0:T(4,128)(2,1)S(1)} all-gather(bf16[96,3,192]{2,1,0:T(4,128)(2,1)S(1)} %copy.82), channel_id=1, replica_groups=mesh['dp'=8,'tp'=4] {'dp'}, dimensions={0}, use_global_device_ids=true | all-gather | bytes 995328 | tf_op jit(solution)/shard_map/all_gather | solution.py:188
  69.6 2.1 copy.83
  71.7 2.0 fusion.110
  76.3 31.1 %all_gather.34 = bf16[192,768]{0,1:T(8,128)(2,1)S(1)} all-gather(bf16[192,96]{0,1:T(8,128)(2,1)S(1)} %copy.85), channel_id=1, replica_groups=mesh['dp'=8,'tp'=4] {'dp'}, dimensions={1}, use_global_device_ids=true | all-gather | bytes 331776 | tf_op jit(solution)/shard_map/all_gather | solution.py:189
  107.4 1.9 fusion.132
  111.6 1.6 fusion.134
  114.0 1.0 broadcast_compare_fusion.1
  115.0 2.3 fusion.107
  118.7 1.2 copy-done
  121.2 1.6 fusion.133
  122.9 1.7 convert_element_type.172
  124.6 1.6 convert_element_type.174
  126.8 32.5 %all-gather.14.cloned.1.call-done = f32[2048,768]{1,0:T(8,128)} async-done(((f32[512,768]{1,0:T(8,128)}), f32[2048,768]{1,0:T(8,128)}) %all-gather.14.cloned.1.call-update) | async-done | bytes 6291472 | tf_op jit(solution)/shard_map/all_gather | solution.py:79
  159.3 4.5 reduce_sum.322
  163.8 44.0 %all-gather.12.cloned.1.call-done = f32[2048,768]{1,0:T(8,128)} async-done(((f32[512,768]{1,0:T(8,128)}), f32[2048,768]{1,0:T(8,128)}) %all-gather.12.cloned.1.call-update) | async-done | bytes 6291472 | tf_op jit(solution)/shard_map/all_gather | solution.py:79
  207.8 4.5 reduce_sum.310
  212.4 2.9 fusion.123
  218.1 33.6 %all-gather.8.cloned.1.call-done = bf16[768,768]{1,0:T(8,128)(2,1)} async-done(((bf16[96,768]{1,0:T(8,128)(2,1)}), bf16[768,768]{1,0:T(8,128)(2,1)}) %all-gather.8.cloned.1.call-update) | async-done | bytes 1179664 | tf_op jit(solution)/shard_map/all_gather | solution.py:190
  251.7 7.6 multiply_convert_fusion.3
  259.3 34.3 %all-gather.10.cloned.1.call-done = bf16[768,768]{0,1:T(8,128)(2,1)} async-done(((bf16[768,96]{0,1:T(8,128)(2,1)}), bf16[768,768]{0,1:T(8,128)(2,1)}) %all-gather.10.cloned.1.call-update) | async-done | bytes 1179664 | tf_op jit(solution)/shard_map/all_gather | solution.py:191
  293.6 3.6 add_convert_fusion.1
  298.1 2.0 fusion.135
  300.1 5.0 multiply_convert_fusion.2
  305.2 1.1 add_convert_fusion
  307.2 2.0 fusion.136
  309.4 1.3 log_add_fusion.1
  311.4 3.3 convolution_convert_fusion.1
  314.8 1.8 convolution_convert_fusion
  316.6 60.2 %all-reduce.5.cloned.1.call-done = (f32[512,768]{1,0:T(8,128)}, f32[512,768]{1,0:T(8,128)}) async-done(((f32[512,768]{1,0:T(8,128)}, f32[512,768]{1,0:T(8,128)}), (f32[512,768]{1,0:T(8,128)}, f32[512,768]{1,0:T(8,128)})) %all-reduce.5.cloned.1.call-update) | async-done | bytes 3145744 | tf_op jit(solution)/shard_map/psum | solution.py:95
  376.8 4.6 multiply_reduce_fusion.3
  381.6 1.4 fusion.120
  385.6 1.0 copy-done.1
  395.3 1.7 bitcast_convert_fusion.1
  397.0 1.7 bitcast_convert_fusion
  398.9 1.2 copy-done.10
  400.2 3.5 fusion.112
  405.6 1.2 copy.110
  407.0 61.1 %all-reduce.7.cloned.1.call-done = (bf16[512,768]{1,0:T(8,128)(2,1)}, bf16[512,768]{1,0:T(8,128)(2,1)}, bf16[512,768]{1,0:T(8,128)(2,1)}, bf16[512,768]{1,0:T(8,128)(2,1)}) async-done(((bf16[512,768]{1,0:T(8,128)(2,1)}, bf16[512,768]{1,0:T(8,128)(2,1)}, bf16[512,768]{1,0:T(8,128)(2,1)}, bf16[512,768]{1,0:T(8,128)(2,1)}), (bf16[512,768]{1,0:T(8,128)(2,1)}, bf16[512,768]{1,0:T(8,128)(2,1)}, ...) | async-done | bytes 3145744 | tf_op jit(solution)/shard_map/psum | solution.py:87
  468.1 2.5 fusion.9
  470.8 2.5 fusion.12
  474.5 4.4 convolution_add_fusion.1
  479.0 2.4 fusion.78
  481.4 2.3 convolution_add_fusion
  484.6 2.1 fusion.71
  486.8 2.5 convolution_add_fusion.2
  489.4 44.6 %reduce-scatter.16.cloned.1.call-done = f32[96,192]{1,0:T(8,128)} async-done(((f32[768,192]{1,0:T(8,128)}), f32[96,192]{1,0:T(8,128)}) %reduce-scatter.16.cloned.1.call-update) | async-done | bytes 73744
  534.0 1.0 copy.111
  535.7 2.7 add_bitcast_fusion.1
  539.5 1.9 pad_maximum_fusion
  543.6 54.5 %reduce-scatter.18.cloned.1.call-done = f32[96,4]{1,0:T(8,128)} async-done(((f32[768,4]{1,0:T(8,128)}), f32[96,4]{1,0:T(8,128)}) %reduce-scatter.18.cloned.1.call-update) | async-done | bytes 1552
  600.2 69.8 %reduce-scatter.12.cloned.1.call-done = f32[96,768]{1,0:T(8,128)} async-done(((f32[768,768]{1,0:T(8,128)}), f32[96,768]{1,0:T(8,128)}) %reduce-scatter.12.cloned.1.call-update) | async-done | bytes 294928 | tf_op jit(solution)/shard_map/reduce_scatter | solution.py:200
  669.9 1.6 multiply_reduce_fusion.9
  671.6 70.1 %reduce-scatter.14.cloned.1.call-done = f32[768,96]{0,1:T(8,128)} async-done(((f32[768,768]{0,1:T(8,128)}), f32[768,96]{0,1:T(8,128)}) %reduce-scatter.14.cloned.1.call-update) | async-done | bytes 294928 | tf_op jit(solution)/shard_map/reduce_scatter | solution.py:201
  741.7 1.6 multiply_reduce_fusion.8
  743.3 70.2 %reduce-scatter.10.cloned.1.call-done = f32[96,3,192]{2,0,1:T(8,128)} async-done(((f32[768,3,192]{2,0,1:T(8,128)}), f32[96,3,192]{2,0,1:T(8,128)}) %reduce-scatter.10.cloned.1.call-update) | async-done | bytes 221200 | tf_op jit(solution)/shard_map/reduce_scatter | solution.py:198
  813.6 1.6 multiply_reduce_fusion.10
  817.9 1.3 pad_maximum_fusion.1
  819.2 39.5 %psum.55 = f32[]{:T(128)} all-reduce(f32[]{:T(128)S(6)} %add.319), channel_id=1, replica_groups=mesh['dp'=8,'tp'=4] {'dp','tp'}, use_global_device_ids=true, to_apply=%region_53.54 | all-reduce | flops 1 | bytes 8 | tf_op jit(solution)/shard_map/psum | solution.py:216
  860.9 1.1 multiply_subtract_fusion
  862.0 1.1 multiply_subtract_fusion.1
  863.1 1.1 multiply_subtract_fusion.2
  (372 shorter events, 38.5 us)
Async XLA Ops:
  7.2 152.1 %all-gather.14.cloned.1.call-start = ((), (), s32[]{:S(2)}) async-start(), calls=%async_computation.8 | async-start | bytes 7864320 | tf_op jit(solution)/shard_map/all_gather | solution.py:79
  8.2 26.0 %copy-start.36 = (f32[96,3,192]{2,0,1:T(8,128)S(1)}, f32[96,3,192]{2,0,1:T(8,128)}, u32[]{:S(2)}) copy-start(f32[96,3,192]{2,0,1:T(8,128)} %param.23) | copy-start | bytes 663556
  10.0 61.7 %copy-start.80 = (f32[512]{0:T(512)}, f32[512]{0:T(512)S(1)}, u32[]{:S(2)}) copy-start(f32[512]{0:T(512)S(1)} %get-tuple-element.106) | copy-start | bytes 6148
  10.0 104.9 %copy-start.82 = (f32[512]{0:T(512)}, f32[512]{0:T(512)S(1)}, u32[]{:S(2)}) copy-start(f32[512]{0:T(512)S(1)} %get-tuple-element.107) | copy-start | bytes 6148
  11.2 22.4 %copy-start.115 = (f32[512]{0:T(512)}, f32[512]{0:T(512)S(1)}, u32[]{:S(2)}) copy-start(f32[512]{0:T(512)S(1)} %get-tuple-element.33) | copy-start | bytes 6148
  11.2 60.5 %copy-start.101 = (f32[512]{0:T(512)}, f32[512]{0:T(512)S(1)}, u32[]{:S(2)}) copy-start(f32[512]{0:T(512)S(1)} %fusion.100) | copy-start | bytes 6148
  34.2 37.5 %copy-start.131 = (f32[768]{0:T(1024)}, f32[768]{0:T(1024)S(1)}, u32[]{:S(2)}) copy-start(f32[768]{0:T(1024)S(1)} %get-tuple-element.40) | copy-start | bytes 9220
  34.2 80.8 %copy-start.72 = (f32[768]{0:T(1024)}, f32[768]{0:T(1024)S(1)}, u32[]{:S(2)}) copy-start(f32[768]{0:T(1024)S(1)} %get-tuple-element.41) | copy-start | bytes 9220
  113.2 94.6 %all-gather.12.cloned.1.call-start = ((), (), s32[]{:S(2)}) async-start(), calls=%async_computation.7 | async-start | bytes 7864320 | tf_op jit(solution)/shard_map/all_gather | solution.py:79
  122.8 128.9 %all-gather.8.cloned.1.call-start = ((), (), s32[]{:S(2)}) async-start(), calls=%async_computation.5 | async-start | bytes 1327104 | tf_op jit(solution)/shard_map/all_gather | solution.py:190
  124.5 169.0 %all-gather.10.cloned.1.call-start = ((), (), s32[]{:S(2)}) async-start(), calls=%async_computation.6 | async-start | bytes 1327104 | tf_op jit(solution)/shard_map/all_gather | solution.py:191
  126.3 250.5 %all-reduce.5.cloned.1.call-start = ((), (), s32[]{:S(2)}) async-start(), calls=%async_computation.14 | async-start | bytes 6291456 | tf_op jit(solution)/shard_map/psum | solution.py:95
  300.1 5.0 copy-start.12
  300.1 5.0 copy-start.136
  309.2 158.9 %all-reduce.7.cloned.1.call-start = ((), (), s32[]{:S(2)}) async-start(), calls=%async_computation.15 | async-start | bytes 6291456 | tf_op jit(solution)/shard_map/psum | solution.py:87
  376.8 4.7 copy-start.120
  376.8 4.7 copy-start.118
  376.8 4.8 copy-start.6
  376.8 4.8 copy-start.9
  376.8 4.8 copy-start.26
  376.8 4.8 copy-start.27
  376.8 4.8 copy-start.78
  376.8 4.8 copy-start.87
  376.8 4.8 copy-start.90
  376.8 4.8 copy-start.95
  376.8 4.8 copy-start.112
  384.7 5.7 copy-start.22
  389.2 5.5 copy-start.65
  389.8 4.9 copy-start.66
  398.8 4.9 copy-start.126
  398.8 4.9 copy-start.125
  398.8 4.9 copy-start.124
  398.9 4.9 copy-start.123
  398.9 4.9 copy-start.25
  398.9 4.9 copy-start.51
  398.9 135.1 %reduce-scatter.16.cloned.1.call-start = ((), (), s32[]{:S(2)}) async-start(), calls=%async_computation.12 | async-start | bytes 884736
  405.5 62.6 %copy-start.3 = (bf16[2,512,768]{2,1,0:T(8,128)(2,1)S(1)}, bf16[2,512,768]{2,1,0:T(8,128)(2,1)}, u32[]{:S(2)}) copy-start(bf16[2,512,768]{2,1,0:T(8,128)(2,1)} %param.19) | copy-start | bytes 4718596
  405.5 62.6 %copy-start.73 = (f32[768]{0:T(1024)S(1)}, f32[768]{0:T(1024)}, u32[]{:S(2)}) copy-start(f32[768]{0:T(1024)} %copy-done.72) | copy-start | bytes 9220
  405.5 62.5 %copy-start.81 = (f32[512]{0:T(512)S(1)}, f32[512]{0:T(512)}, u32[]{:S(2)}) copy-start(f32[512]{0:T(512)} %copy-done.80) | copy-start | bytes 6148
  405.5 62.5 %copy-start.83 = (f32[512]{0:T(512)S(1)}, f32[512]{0:T(512)}, u32[]{:S(2)}) copy-start(f32[512]{0:T(512)} %copy-done.82) | copy-start | bytes 6148
  406.7 191.3 %reduce-scatter.18.cloned.1.call-start = ((), (), s32[]{:S(2)}) async-start(), calls=%async_computation.13 | async-start | bytes 442368
  474.4 195.5 %reduce-scatter.12.cloned.1.call-start = ((), (), s32[]{:S(2)}) async-start(), calls=%async_computation.10 | async-start | bytes 2654208 | tf_op jit(solution)/shard_map/reduce_scatter | solution.py:200
  478.9 262.8 %reduce-scatter.14.cloned.1.call-start = ((), (), s32[]{:S(2)}) async-start(), calls=%async_computation.11 | async-start | bytes 2654208 | tf_op jit(solution)/shard_map/reduce_scatter | solution.py:201
  483.7 329.9 %reduce-scatter.10.cloned.1.call-start = ((), (), s32[]{:S(2)}) async-start(), calls=%async_computation.9 | async-start | bytes 2654208 | tf_op jit(solution)/shard_map/reduce_scatter | solution.py:198
  489.3 46.3 %copy-start.128 = (f32[512]{0:T(512)S(1)}, f32[512]{0:T(512)}, u32[]{:S(2)}) copy-start(f32[512]{0:T(512)} %get-tuple-element.25) | copy-start | bytes 6148
  489.3 46.3 %copy-start.127 = (f32[512]{0:T(512)S(1)}, f32[512]{0:T(512)}, u32[]{:S(2)}) copy-start(f32[512]{0:T(512)} %get-tuple-element.26) | copy-start | bytes 6148
  489.3 46.3 %copy-start.84 = (f32[512]{0:T(512)S(1)}, f32[512]{0:T(512)}, u32[]{:S(2)}) copy-start(f32[512]{0:T(512)} %copy-done.82) | copy-start | bytes 6148
  489.3 46.3 %copy-start.100 = (f32[512]{0:T(512)S(1)}, f32[512]{0:T(512)}, u32[]{:S(2)}) copy-start(f32[512]{0:T(512)} %copy-done.99) | copy-start | bytes 6148
  489.3 46.3 %copy-start.107 = (f32[512]{0:T(512)S(1)}, f32[512]{0:T(512)}, u32[]{:S(2)}) copy-start(f32[512]{0:T(512)} %copy-done.105) | copy-start | bytes 6148
  489.3 46.3 %copy-start.111 = (f32[512]{0:T(512)S(1)}, f32[512]{0:T(512)}, u32[]{:S(2)}) copy-start(f32[512]{0:T(512)} %copy-done.110) | copy-start | bytes 6148
  817.8 41.6 %copy-start.130 = (f32[4,96]{1,0:T(4,128)S(1)}, f32[4,96]{1,0:T(4,128)}, u32[]{:S(2)}) copy-start(f32[4,96]{1,0:T(4,128)} %param.27) | copy-start | bytes 4612
  817.8 41.6 %copy-start.134 = (f32[4,96]{1,0:T(4,128)S(1)}, f32[4,96]{1,0:T(4,128)}, u32[]{:S(2)}) copy-start(f32[4,96]{1,0:T(4,128)} %param.32) | copy-start | bytes 4612
  817.8 41.6 %copy-start.135 = (f32[4,96]{1,0:T(4,128)S(1)}, f32[4,96]{1,0:T(4,128)}, u32[]{:S(2)}) copy-start(f32[4,96]{1,0:T(4,128)} %param.37) | copy-start | bytes 4612
  817.8 42.2 %copy-start.56 = (f32[192,96]{1,0:T(8,128)S(1)}, f32[192,96]{1,0:T(8,128)}, u32[]{:S(2)}) copy-start(f32[192,96]{1,0:T(8,128)} %param.24) | copy-start | bytes 221188
  817.9 42.2 %copy-start.74 = (f32[192,96]{1,0:T(8,128)S(1)}, f32[192,96]{1,0:T(8,128)}, u32[]{:S(2)}) copy-start(f32[192,96]{1,0:T(8,128)} %param.29) | copy-start | bytes 221188
  817.9 42.2 %copy-start.75 = (f32[192,96]{1,0:T(8,128)S(1)}, f32[192,96]{1,0:T(8,128)}, u32[]{:S(2)}) copy-start(f32[192,96]{1,0:T(8,128)} %param.34) | copy-start | bytes 221188
  817.9 43.0 %copy-start.34 = (f32[768,96]{0,1:T(8,128)S(1)}, f32[768,96]{0,1:T(8,128)}, u32[]{:S(2)}) copy-start(f32[768,96]{0,1:T(8,128)} %param.26) | copy-start | bytes 884740
  817.9 43.0 %copy-start.39 = (f32[768,96]{0,1:T(8,128)S(1)}, f32[768,96]{0,1:T(8,128)}, u32[]{:S(2)}) copy-start(f32[768,96]{0,1:T(8,128)} %reduce-scatter.14.cloned.1.call-done) | copy-start | bytes 884740
  817.9 43.0 %copy-start.57 = (f32[768,96]{0,1:T(8,128)S(1)}, f32[768,96]{0,1:T(8,128)}, u32[]{:S(2)}) copy-start(f32[768,96]{0,1:T(8,128)} %param.31) | copy-start | bytes 884740
  817.9 42.9 %copy-start.58 = (f32[768,96]{0,1:T(8,128)S(1)}, f32[768,96]{0,1:T(8,128)}, u32[]{:S(2)}) copy-start(f32[768,96]{0,1:T(8,128)} %param.36) | copy-start | bytes 884740
  819.2 42.8 %copy-start.35 = (f32[96,768]{1,0:T(8,128)S(1)}, f32[96,768]{1,0:T(8,128)}, u32[]{:S(2)}) copy-start(f32[96,768]{1,0:T(8,128)} %param.25) | copy-start | bytes 884740
  819.2 42.8 %copy-start.38 = (f32[96,768]{1,0:T(8,128)S(1)}, f32[96,768]{1,0:T(8,128)}, u32[]{:S(2)}) copy-start(f32[96,768]{1,0:T(8,128)} %reduce-scatter.12.cloned.1.call-done) | copy-start | bytes 884740
  819.2 42.8 %copy-start.59 = (f32[96,768]{1,0:T(8,128)S(1)}, f32[96,768]{1,0:T(8,128)}, u32[]{:S(2)}) copy-start(f32[96,768]{1,0:T(8,128)} %param.30) | copy-start | bytes 884740
  819.2 42.8 %copy-start.60 = (f32[96,768]{1,0:T(8,128)S(1)}, f32[96,768]{1,0:T(8,128)}, u32[]{:S(2)}) copy-start(f32[96,768]{1,0:T(8,128)} %param.35) | copy-start | bytes 884740
  (87 other events, 177.9 us)
Sparse Core Ops, SparseCore 0:
  113.3 45.8 all-gather.13
  161.4 46.3 all-gather.11
  210.6 41.0 all-gather.7
  253.7 39.8 all-gather.9
  309.3 67.4 all-reduce.4
  398.9 69.0 all-reduce.6
  471.4 62.5 reduce-scatter.15
  537.6 60.3 reduce-scatter.17
  601.9 67.9 reduce-scatter.11
  673.7 67.9 reduce-scatter.13
  745.6 67.9 reduce-scatter.9
